TPU v7x, 128 devices: a whole 4x4x4 slice. The times are simulated.
128 devices in a mesh: dp: 8 (over y, core), prompt: 16 (over x, z).
Axes of the slice: x: 4, y: 4, z: 4, core: 2. Of those that a mesh axis runs over, the one named last changes fastest.
Arguments:
- cand_hidden: bfloat16 [16, 8, 128, 1024], P('prompt', 'dp')
- ref_hidden: bfloat16 [32, 16, 128, 1024], P('dp', 'prompt')
- cand_ids: int32 [16, 8, 128], P('prompt', 'dp'), may hold values from 0 to 50264
- ref_ids: int32 [32, 16, 128], P('dp', 'prompt'), may hold values from 0 to 50264
- cand_len: int32 [16, 8], P('prompt', 'dp'), may hold values from 32 to 128
- reference_length: int32 [32, 16], P('dp', 'prompt'), may hold values from 32 to 128
- idf_table: float32 [50265], replicated, may hold values from 1 to 10
- up_weight: bfloat16 [1024, 4096], replicated, may hold values from -0.1875 to 0.1875
- up_bias: float32 [4096], replicated, may hold values from -3 to 3
- down_weight: bfloat16 [4096, 1024], replicated, may hold values from -0.09375 to 0.09375
- down_bias: float32 [1024], replicated, may hold values from -3 to 3
- norm_gain: float32 [1024], replicated, may hold values from 0.3 to 3
- norm_bias: float32 [1024], replicated, may hold values from -3 to 3
- pair_cand: int32 [8, 16, 32], P('dp', 'prompt'), may hold values from 0 to 7
- pair_ref: int32 [8, 16, 32], P('dp', 'prompt'), may hold values from 0 to 63
- pair_count: int32 [8, 16], P('dp', 'prompt'), may hold values from 8 to 32, as said below
Outputs:
- pair_scores: float32 [3, 8, 16, 32], P(None, 'dp', 'prompt')
- totals: float32 [3], replicated
Inputs may be any that keep to these rules, and one draw needn't show every extreme that they name: Slots from pair_count on are not live; some device has all 32 slots live.
All inputs are finite; a program needn't handle non-finite values.
Results may differ from a plain program's by a relative error of at most 0.0003.
Values may be sent and summed in bfloat16 or wider, within the bound.
No kernel may reach another device: no remote copies, remote signals or barrier semaphores. Data moves between devices by JAX's collectives and lax.ppermute only.
A program may use at most 128 MiB of HBM per device.

v0:
```python
import jax
import jax.numpy as jnp
from jax import lax
from jax.sharding import PartitionSpec as P


def encode_rows(hidden, up_weight, up_bias, down_weight, down_bias, norm_gain, norm_bias):
    preactivation_hidden = jnp.dot(hidden, up_weight, preferred_element_type=jnp.float32) + up_bias
    activated = jax.nn.gelu(preactivation_hidden, approximate=False).astype(jnp.bfloat16)
    summed = (
        hidden.astype(jnp.float32)
        + jnp.dot(activated, down_weight, preferred_element_type=jnp.float32)
        + down_bias
    )
    center = jnp.mean(summed, axis=-1, keepdims=True)
    spread = jnp.mean(jnp.square(summed - center), axis=-1, keepdims=True)
    normed = (summed - center) * lax.rsqrt(spread + 1e-05) * norm_gain + norm_bias
    magnitude = jnp.sum(jnp.square(normed), axis=-1, keepdims=True)
    return (normed * lax.rsqrt(magnitude + 1e-06)).astype(jnp.bfloat16)


def token_idf_weights(ids, lengths, idf_table):
    positions = jnp.arange(ids.shape[-1], dtype=jnp.int32)
    live_tokens = positions[None, :] < lengths[:, None]
    return jnp.where(live_tokens, jnp.take(idf_table, ids, axis=0), 0.0).astype(jnp.bfloat16)


def on_device(
    cand_hidden,
    ref_hidden,
    cand_ids,
    ref_ids,
    cand_len,
    reference_length,
    idf_table,
    up_weight,
    up_bias,
    down_weight,
    down_bias,
    norm_gain,
    norm_bias,
    pair_cand,
    pair_ref,
    pair_count,
):
    seq_len = cand_hidden.shape[2]
    width = cand_hidden.shape[3]

    def encode_side(hidden, ids, lengths):
        units = encode_rows(
            hidden.reshape(-1, width),
            up_weight,
            up_bias,
            down_weight,
            down_bias,
            norm_gain,
            norm_bias,
        )
        weights = token_idf_weights(ids.reshape(-1, seq_len), lengths.reshape(-1), idf_table)
        return (units.reshape(hidden.shape), weights.reshape(hidden.shape[:3]))

    ref_unit, ref_weight = encode_side(ref_hidden, ref_ids, reference_length)
    candidate_normalized, cand_weight = encode_side(cand_hidden, cand_ids, cand_len)
    cand_all, cand_wall = (
        lax.all_gather(candidate_normalized, "dp", axis=1, tiled=True),
        lax.all_gather(cand_weight, "dp", axis=1, tiled=True),
    )
    cand_all = cand_all.reshape(-1, seq_len, width)
    cand_wall = cand_wall.reshape(-1, seq_len)
    cand_pick = pair_cand.reshape(-1)
    slot_total = cand_pick.shape[0]
    ref_pick = pair_ref.reshape(-1)
    groups = lax.axis_size("prompt")
    ref_major = ref_pick // groups
    ref_minor = ref_pick % groups
    order = jnp.argsort(ref_minor, stable=True)
    sorted_minor = jnp.take(ref_minor, order, axis=0)
    sorted_major = jnp.take(ref_major, order, axis=0)
    sorted_cand = jnp.take(cand_pick, order, axis=0)
    paired_normalized = jnp.take(cand_all, sorted_cand, axis=0)
    pair_weight = jnp.take(cand_wall, sorted_cand, axis=0)
    initial = (
        jnp.zeros((slot_total, seq_len), jnp.float32),
        jnp.zeros((slot_total, seq_len), jnp.float32),
        jnp.zeros((slot_total, seq_len), jnp.bfloat16),
    )
    ref_all, ref_wall = (
        lax.all_gather(ref_unit, "prompt", axis=1, tiled=True),
        lax.all_gather(ref_weight, "prompt", axis=1, tiled=True),
    )
    shard_span = ref_all.shape[1]
    inside = (sorted_minor >= 0) & (sorted_minor < 0 + shard_span)
    within = sorted_major * shard_span + jnp.clip(sorted_minor - 0, 0, shard_span - 1)
    selected_normalized = jnp.take(ref_all.reshape(-1, seq_len, width), within, axis=0)
    chosen_weight = jnp.take(ref_wall.reshape(-1, seq_len), within, axis=0)
    cosine_similarity = jnp.einsum(
        "uqg,uog->uqo", paired_normalized, selected_normalized, preferred_element_type=jnp.float32
    )
    row_best = jnp.max(
        jnp.where(chosen_weight[:, None, :] > 0, cosine_similarity, -10000.0), axis=2
    )
    col_best = jnp.max(jnp.where(pair_weight[:, :, None] > 0, cosine_similarity, -10000.0), axis=1)
    keeper = inside[:, None]
    updated = []
    for stored, fresh in zip(initial, (row_best, col_best, chosen_weight)):
        updated.append(jnp.where(keeper, fresh, stored))
    row_best, col_best, ref_chosen = tuple(updated)
    cand_float = pair_weight.astype(jnp.float32)
    ref_float = ref_chosen.astype(jnp.float32)
    precision_sorted = jnp.sum(cand_float * row_best, axis=1) / jnp.sum(cand_float, axis=1)
    recall_sorted = jnp.sum(ref_float * col_best, axis=1) / jnp.sum(ref_float, axis=1)
    inverse = jnp.argsort(order)
    precision = jnp.take(precision_sorted, inverse, axis=0)
    recall = jnp.take(recall_sorted, inverse, axis=0)
    fmeasure = 2.0 * precision * recall / jnp.maximum(precision + recall, 0.7)
    live_slots = jnp.arange(slot_total, dtype=jnp.int32) < pair_count.reshape(1)
    stacked = jnp.where(live_slots[None, :], jnp.stack([precision, recall, fmeasure]), 0.0)
    score_sums, live_total = lax.psum(
        (jnp.sum(stacked, axis=1), jnp.sum(live_slots.astype(jnp.float32))), ("dp", "prompt")
    )
    return (stacked.reshape(3, 1, 1, slot_total), score_sums / live_total)


def solution(mesh):
    placed = (
        P("prompt", "dp", None, None),
        P("dp", "prompt", None, None),
        P("prompt", "dp", None),
        P("dp", "prompt", None),
        P("prompt", "dp"),
        P("dp", "prompt"),
        P(),
        P(),
        P(),
        P(),
        P(),
        P(),
        P(),
        P("dp", "prompt", None),
        P("dp", "prompt", None),
        P("dp", "prompt"),
    )
    return jax.shard_map(
        on_device,
        mesh=mesh,
        in_specs=placed,
        out_specs=(P(None, "dp", "prompt", None), P()),
        check_vma=False,
    )
```

profile of v0, /device:TPU:1, one launch (start us, length us, event | category | flops | bytes accessed | tf_op | source)
XLA Modules:
  0.0 263.4 jit_solution(12290140118969234346)
XLA Ops:
  7.2 13.2 %fusion.169 = (f32[128]{0:T(128)S(1)}, f32[128,1024]{1,0:T(8,128)S(1)}) fusion(f32[1024]{0:T(1024)} %param.30, bf16[4096,1024]{1,0:T(8,128)(2,1)} %param.29, bf16[1024,4096]{1,0:T(8,128)(2,1)} %param.27, f32[4096]{0:T(1024)} %param.28, bf16[1,1,128,1024]{3,2,1,0:T(8,128)(2,1)} %param.20), kind=kOutput, calls=%fused_computation.264 | convolution fusion | flops 2182610944 | bytes 17584640 | tf_op jit(solution)/shard_map/dot_general | solution.py:12
  20.5 0.2 multiply_reduce_fusion.3
  20.7 0.3 multiply_reduce_fusion.2
  21.0 0.9 multiply_convert_fusion.1
  21.9 0.2 all-gather.4.cloned.1.call-start
  22.2 30.3 %fusion.168 = (f32[512]{0:T(512)S(1)}, f32[512,1024]{1,0:T(8,128)S(1)}) fusion(f32[1024]{0:T(1024)S(1)} %copy-done.9, bf16[4096,1024]{1,0:T(8,128)(2,1)} %param.29, bf16[512,1024]{1,0:T(8,128)(2,1)S(1)} %bitcast.84, bf16[1024,4096]{1,0:T(8,128)(2,1)} %param.27, f32[4096]{0:T(1024)S(1)} %copy-done.8), kind=kOutput, calls=%fused_computation.263 | convolution fusion | flops 8730443776 | bytes 19945472 | tf_op jit(solution)/shard_map/dot_general | solution.py:12
  52.5 0.4 multiply_reduce_fusion.1
  52.8 0.9 multiply_reduce_fusion
  53.8 1.5 multiply_convert_fusion
  56.6 1.1 gather_fusion
  57.8 12.1 %all_gather.12 = bf16[1,8,128]{2,0,1:T(2,128)(2,1)S(1)} all-gather(bf16[1,1,128]{2,0,1:T(2,128)(2,1)S(1)} %fusion.100), channel_id=1, replica_groups=mesh['dp'=8,'prompt'=16] {'dp'}, dimensions={1}, use_global_device_ids=true | all-gather | bytes 2304 | tf_op jit(solution)/shard_map/all_gather | solution.py:66
  69.9 1.6 sort.34
  71.5 0.7 gather_fusion.7
  72.2 0.7 gather_fusion.8
  72.9 0.7 gather_fusion.6
  73.6 3.1 %gather_fusion.2 = bf16[512]{0:T(512)(128)(2,1)S(1)} fusion(f32[50265]{0:T(1024)S(1)} %copy-done, s32[1024]{0:T(1024)S(1)} %pad_clamp_fusion.2), kind=kCustom, calls=%fused_computation.7 | custom fusion | bytes 4096 | tf_op jit(solution)/shard_map/jit(_take)/gather | solution.py:25
  76.8 20.3 %all_gather.13 = bf16[4,16,128]{2,0,1:T(4,128)(2,1)S(1)} all-gather(bf16[4,1,128]{2,0,1:T(4,128)(2,1)S(1)} %fusion.98), channel_id=1, replica_groups=mesh['dp'=8,'prompt'=16] {'prompt'}, dimensions={1}, use_global_device_ids=true | all-gather | bytes 17408 | tf_op jit(solution)/shard_map/all_gather | solution.py:89
  97.2 1.6 sort.35
  98.8 0.6 convert_reduce_fusion.2
  99.4 0.6 gather_fusion.1
  100.0 0.6 gather_fusion.3
  100.8 6.9 %gather_fusion.4 = bf16[32,128,1024]{2,1,0:T(8,128)(2,1)} fusion(bf16[8,128,1024]{2,1,0:T(8,128)(2,1)} %bitcast.74, s32[1024]{0:T(1024)S(1)} %get-tuple-element.39), kind=kCustom, calls=%fused_computation.9 | custom fusion | bytes 16777344 | tf_op jit(solution)/shard_map/jit(_take)/gather | solution.py:80
  107.7 62.4 %all-gather.4.cloned.1.call-done = bf16[4,16,128,1024]{3,2,1,0:T(8,128)(2,1)} async-done(((bf16[4,1,128,1024]{3,2,1,0:T(8,128)(2,1)}), bf16[4,16,128,1024]{3,2,1,0:T(8,128)(2,1)}) %all-gather.4.cloned.1.call-update) | async-done | bytes 16777232 | tf_op jit(solution)/shard_map/all_gather | solution.py:88
  170.1 10.8 %gather_fusion.5 = bf16[32,128,1024]{2,1,0:T(8,128)(2,1)} fusion(bf16[64,128,1024]{2,1,0:T(8,128)(2,1)} %bitcast.75, s32[1024]{0:T(1024)S(1)} %get-tuple-element.38), kind=kCustom, calls=%fused_computation.10 | custom fusion | bytes 16777344 | tf_op jit(solution)/shard_map/jit(_take)/gather | solution.py:94
  180.8 7.5 %select_reduce_fusion = (f32[32,128]{1,0:T(8,128)S(1)}, f32[32,128]{1,0:T(8,128)S(1)}) fusion(pred[32,128]{1,0:T(8,128)(4,1)S(1)} %broadcast_compare_fusion, pred[32,128]{1,0:T(8,128)(4,1)S(1)} %broadcast_compare_fusion.1, bf16[32,128,1024]{2,1,0:T(8,128)(2,1)} %gather_fusion.5, pred[32]{0:T(512)(128)(4,1)S(1)} %get-tuple-element.22, ...), kind=kOutput, calls=%fused_computation.73 | convolution fusion | flops 1084219392 | bytes 16818240 | tf_op jit(solution)/shard_map/uqg,uog->uqo/dot_general | solution.py:96
  188.4 0.2 convert_reduce_fusion.1
  188.6 0.7 gather_fusion.9
  189.3 0.7 gather_fusion.10
  190.1 0.1 fusion.96
  190.2 64.7 %all-reduce = (f32[3]{0:T(128)S(1)}, f32[]{:T(128)}) all-reduce(f32[3]{0:T(128)S(1)} %fusion.96, f32[]{:T(128)} %convert_reduce_fusion.2), channel_id=1, replica_groups=mesh['dp'=8,'prompt'=16] {'dp','prompt'}, use_global_device_ids=true, to_apply=%region_15.18 | all-reduce | flops 4 | bytes 32 | tf_op jit(solution)/shard_map/psum | solution.py:118
  254.9 1.2 broadcast_divide_fusion
  256.0 0.6 broadcast_select_fusion.3
  (57 shorter events, 0.5 us)
Async XLA Ops:
  7.2 49.4 %copy-start = (f32[50265]{0:T(1024)S(1)}, f32[50265]{0:T(1024)}, u32[]{:S(2)}) copy-start(f32[50265]{0:T(1024)} %param.26) | copy-start | bytes 603184
  7.2 13.5 %copy-start.2 = (f32[1024]{0:T(1024)S(1)}, f32[1024]{0:T(1024)}, u32[]{:S(2)}) copy-start(f32[1024]{0:T(1024)} %param.32) | copy-start | bytes 12292
  7.2 13.5 %copy-start.3 = (f32[1024]{0:T(1024)S(1)}, f32[1024]{0:T(1024)}, u32[]{:S(2)}) copy-start(f32[1024]{0:T(1024)} %param.31) | copy-start | bytes 12292
  7.2 93.6 %all-gather.6.cloned.1.call-start = ((), (), s32[]{:S(2)}) async-start(), calls=%async_computation.1 | async-start | bytes 2359296 | tf_op jit(solution)/shard_map/all_gather | solution.py:65
  20.5 1.7 copy-start.7
  20.5 1.7 copy-start.8
  20.5 1.7 copy-start.9
  21.9 148.1 %all-gather.4.cloned.1.call-start = ((), (), s32[]{:S(2)}) async-start(), calls=%async_computation | async-start | bytes 17825792 | tf_op jit(solution)/shard_map/all_gather | solution.py:88
  53.7 2.8 %copy-start.6 = (s32[1,1,128]{2,1,0:T(1,128)S(1)}, s32[1,1,128]{2,1,0:T(1,128)}, u32[]{:S(2)}) copy-start(s32[1,1,128]{2,1,0:T(1,128)} %param.22) | copy-start | bytes 1540
  53.7 16.1 %copy-start.10 = (s32[1,1,32]{2,1,0:T(1,128)S(1)}, s32[1,1,32]{2,1,0:T(1,128)}, u32[]{:S(2)}) copy-start(s32[1,1,32]{2,1,0:T(1,128)} %param.34) | copy-start | bytes 388
  55.2 17.7 %copy-start.1 = (s32[1,1,32]{2,1,0:T(1,128)S(1)}, s32[1,1,32]{2,1,0:T(1,128)}, u32[]{:S(2)}) copy-start(s32[1,1,32]{2,1,0:T(1,128)} %param.33) | copy-start | bytes 388
  55.2 18.4 %copy-start.4 = (s32[4,1,128]{2,1,0:T(1,128)S(1)}, s32[4,1,128]{2,1,0:T(1,128)}, u32[]{:S(2)}) copy-start(s32[4,1,128]{2,1,0:T(1,128)} %param.23) | copy-start | bytes 6148
  55.2 21.6 %copy-start.5 = (s32[4,1]{0,1:T(1,128)S(1)}, s32[4,1]{0,1:T(1,128)}, u32[]{:S(2)}) copy-start(s32[4,1]{0,1:T(1,128)} %param.25) | copy-start | bytes 52
Sparse Core Ops, SparseCore 0:
  22.0 28.8 all-gather.5
  55.4 114.6 all-gather.3
where the time goes:
time: 264 us; the launch traced here: 263 us
  blocking collectives  97 us (37%)
  waiting for transfers between devices  62.4 us (24%)
  matrix products  51 us (19%)
  local copies, waits for them, and re-layouts  26.7 us (10%)
  between operations  15.6 us (6%)
  other arithmetic  10.3 us (4%)
    psum x1, blocking collectives, on_device(): lax.psum((jnp.sum(stacked, axis=1), jnp.sum(live_slots.astype(jnp.float32...  64.7 us
    all_gather x1, waiting for transfers between devices, on_device(): lax.all_gather(ref_unit, 'prompt', axis=1, tiled=True)  62.4 us
    dot_general x2, matrix products, encode_rows(): jnp.dot(activated, down_weight, preferred_element_type=jnp.float32)  43.5 us
    all_gather x1, blocking collectives, on_device(): lax.all_gather(ref_weight, 'prompt', axis=1, tiled=True)  20.3 us
    all_gather x1, blocking collectives, on_device(): lax.all_gather(cand_weight, 'dp', axis=1, tiled=True)  12.1 us
    gather x1, local copies, waits for them, and re-layouts, on_device(): jnp.take(ref_all.reshape(-1, seq_len, width), within, axis=0)  10.8 us
    dot_general x1, matrix products, on_device(): jnp.einsum('uqg,uog->uqo', paired_normalized, selected_normalized, prefer...  7.55 us
    gather x1, local copies, waits for them, and re-layouts, on_device(): paired_normalized = jnp.take(cand_all, sorted_cand, axis=0)  6.87 us
  transfers between devices with their start and end apart: 2, of which 1 were waited for; matrix products, arithmetic and copies ran while one was open for 20% of the time, Pallas kernels for 0%

commit v1 on v0

--- a/solution.py
+++ b/solution.py
@@ -116,7 +116,8 @@
     live_slots = jnp.arange(slot_total, dtype=jnp.int32) < pair_count.reshape(1)
     stacked = jnp.where(live_slots[None, :], jnp.stack([precision, recall, fmeasure]), 0.0)
     score_sums, live_total = lax.psum(
-        (jnp.sum(stacked, axis=1), jnp.sum(live_slots.astype(jnp.float32))), ("dp", "prompt")
+        lax.psum((jnp.sum(stacked, axis=1), jnp.sum(live_slots.astype(jnp.float32))), "dp"),
+        "prompt",
     )
     return (stacked.reshape(3, 1, 1, slot_total), score_sums / live_total)
 

time: 264 us -> 253 us (0.958)
  the two profiles are of different devices: /device:TPU:1 before, /device:TPU:0 now
where the time goes in v1:
time: 253 us; the launch traced here: 252 us
  blocking collectives  89.8 us (35%)
  waiting for transfers between devices  58.8 us (23%)
  matrix products  51 us (20%)
  local copies, waits for them, and re-layouts  26.5 us (10%)
  between operations  15.6 us (6%)
  other arithmetic  10.3 us (4%)
    all_gather x1, waiting for transfers between devices, on_device(): lax.all_gather(ref_unit, 'prompt', axis=1, tiled=True)  58.7 us
    dot_general x2, matrix products, encode_rows(): jnp.dot(activated, down_weight, preferred_element_type=jnp.float32)  43.5 us
    psum x1, blocking collectives, on_device(): lax.psum(lax.psum((jnp.sum(stacked, axis=1), jnp.sum(live_slots.astype(jn...  39.5 us
    all_gather x1, blocking collectives, on_device(): lax.all_gather(ref_weight, 'prompt', axis=1, tiled=True)  24.6 us
    psum x1, blocking collectives, on_device(): lax.psum((jnp.sum(stacked, axis=1), jnp.sum(live_slots.astype(jnp.float32...  14.8 us
    all_gather x1, blocking collectives, on_device(): lax.all_gather(cand_weight, 'dp', axis=1, tiled=True)  10.8 us
    gather x1, local copies, waits for them, and re-layouts, on_device(): jnp.take(ref_all.reshape(-1, seq_len, width), within, axis=0)  10.8 us
    dot_general x1, matrix products, on_device(): jnp.einsum('uqg,uog->uqo', paired_normalized, selected_normalized, prefer...  7.55 us
  transfers between devices with their start and end apart: 2, of which 1 were waited for; matrix products, arithmetic and copies ran while one was open for 20% of the time, Pallas kernels for 0%

profile of v1, /device:TPU:0, one launch (start us, length us, event | category | flops | bytes accessed | tf_op | source)
XLA Modules:
  0.0 252.3 jit_solution(9200794824276743782)
XLA Ops:
  7.2 13.2 %fusion.169 = (f32[128]{0:T(128)S(1)}, f32[128,1024]{1,0:T(8,128)S(1)}) fusion(f32[1024]{0:T(1024)} %param.30, bf16[4096,1024]{1,0:T(8,128)(2,1)} %param.29, bf16[1024,4096]{1,0:T(8,128)(2,1)} %param.27, f32[4096]{0:T(1024)} %param.28, bf16[1,1,128,1024]{3,2,1,0:T(8,128)(2,1)} %param.20), kind=kOutput, calls=%fused_computation.264 | convolution fusion | flops 2182610944 | bytes 17584640 | tf_op jit(solution)/shard_map/dot_general | solution.py:12
  20.5 0.2 multiply_reduce_fusion.3
  20.7 0.3 multiply_reduce_fusion.2
  21.0 0.9 multiply_convert_fusion.1
  21.9 0.2 all-gather.4.cloned.1.call-start
  22.2 30.3 %fusion.168 = (f32[512]{0:T(512)S(1)}, f32[512,1024]{1,0:T(8,128)S(1)}) fusion(f32[1024]{0:T(1024)S(1)} %copy-done.9, bf16[4096,1024]{1,0:T(8,128)(2,1)} %param.29, bf16[512,1024]{1,0:T(8,128)(2,1)S(1)} %bitcast.84, bf16[1024,4096]{1,0:T(8,128)(2,1)} %param.27, f32[4096]{0:T(1024)S(1)} %copy-done.8), kind=kOutput, calls=%fused_computation.263 | convolution fusion | flops 8730443776 | bytes 19945472 | tf_op jit(solution)/shard_map/dot_general | solution.py:12
  52.5 0.3 multiply_reduce_fusion.1
  52.8 0.9 multiply_reduce_fusion
  53.7 1.5 multiply_convert_fusion
  56.6 1.1 gather_fusion
  57.8 10.8 %all_gather.12 = bf16[1,8,128]{2,0,1:T(2,128)(2,1)S(1)} all-gather(bf16[1,1,128]{2,0,1:T(2,128)(2,1)S(1)} %fusion.100), channel_id=1, replica_groups=mesh['dp'=8,'prompt'=16] {'dp'}, dimensions={1}, use_global_device_ids=true | all-gather | bytes 2304 | tf_op jit(solution)/shard_map/all_gather | solution.py:66
  68.6 1.6 sort.34
  70.2 0.7 gather_fusion.7
  70.9 0.7 gather_fusion.8
  71.6 0.7 gather_fusion.6
  72.4 3.1 %gather_fusion.2 = bf16[512]{0:T(512)(128)(2,1)S(1)} fusion(f32[50265]{0:T(1024)S(1)} %copy-done, s32[1024]{0:T(1024)S(1)} %pad_clamp_fusion.2), kind=kCustom, calls=%fused_computation.7 | custom fusion | bytes 4096 | tf_op jit(solution)/shard_map/jit(_take)/gather | solution.py:25
  75.6 24.6 %all_gather.13 = bf16[4,16,128]{2,0,1:T(4,128)(2,1)S(1)} all-gather(bf16[4,1,128]{2,0,1:T(4,128)(2,1)S(1)} %fusion.98), channel_id=1, replica_groups=mesh['dp'=8,'prompt'=16] {'prompt'}, dimensions={1}, use_global_device_ids=true | all-gather | bytes 17408 | tf_op jit(solution)/shard_map/all_gather | solution.py:89
  100.2 1.6 sort.35
  101.8 0.6 convert_reduce_fusion.2
  102.5 0.6 gather_fusion.1
  103.1 0.6 gather_fusion.3
  103.9 6.7 %gather_fusion.4 = bf16[32,128,1024]{2,1,0:T(8,128)(2,1)} fusion(bf16[8,128,1024]{2,1,0:T(8,128)(2,1)} %bitcast.74, s32[1024]{0:T(1024)S(1)} %get-tuple-element.41), kind=kCustom, calls=%fused_computation.9 | custom fusion | bytes 16777344 | tf_op jit(solution)/shard_map/jit(_take)/gather | solution.py:80
  110.6 58.7 %all-gather.4.cloned.1.call-done = bf16[4,16,128,1024]{3,2,1,0:T(8,128)(2,1)} async-done(((bf16[4,1,128,1024]{3,2,1,0:T(8,128)(2,1)}), bf16[4,16,128,1024]{3,2,1,0:T(8,128)(2,1)}) %all-gather.4.cloned.1.call-update) | async-done | bytes 16777232 | tf_op jit(solution)/shard_map/all_gather | solution.py:88
  169.3 10.8 %gather_fusion.5 = bf16[32,128,1024]{2,1,0:T(8,128)(2,1)} fusion(bf16[64,128,1024]{2,1,0:T(8,128)(2,1)} %bitcast.75, s32[1024]{0:T(1024)S(1)} %get-tuple-element.40), kind=kCustom, calls=%fused_computation.10 | custom fusion | bytes 16777344 | tf_op jit(solution)/shard_map/jit(_take)/gather | solution.py:94
  180.1 7.5 %select_reduce_fusion = (f32[32,128]{1,0:T(8,128)S(1)}, f32[32,128]{1,0:T(8,128)S(1)}) fusion(pred[32,128]{1,0:T(8,128)(4,1)S(1)} %broadcast_compare_fusion, pred[32,128]{1,0:T(8,128)(4,1)S(1)} %broadcast_compare_fusion.1, bf16[32,128,1024]{2,1,0:T(8,128)(2,1)} %gather_fusion.5, pred[32]{0:T(512)(128)(4,1)S(1)} %get-tuple-element.24, ...), kind=kOutput, calls=%fused_computation.73 | convolution fusion | flops 1084219392 | bytes 16818240 | tf_op jit(solution)/shard_map/uqg,uog->uqo/dot_general | solution.py:96
  187.6 0.2 convert_reduce_fusion.1
  187.9 0.7 gather_fusion.9
  188.6 0.7 gather_fusion.10
  189.4 14.8 %all-reduce.1 = (f32[3]{0:T(128)S(1)}, f32[]{:T(128)}) all-reduce(f32[3]{0:T(128)S(1)} %fusion.96, f32[]{:T(128)} %convert_reduce_fusion.2), channel_id=1, replica_groups=mesh['dp'=8,'prompt'=16] {'dp'}, use_global_device_ids=true, to_apply=%region_15.18 | all-reduce | flops 4 | bytes 32 | tf_op jit(solution)/shard_map/psum | solution.py:119
  204.2 39.5 %all-reduce = (f32[3]{0:T(128)S(1)}, f32[]{:T(128)}) all-reduce(f32[3]{0:T(128)S(1)} %get-tuple-element.18, f32[]{:T(128)} %get-tuple-element.19), channel_id=1, replica_groups=mesh['dp'=8,'prompt'=16] {'prompt'}, use_global_device_ids=true, to_apply=%region_16.19 | all-reduce | flops 4 | bytes 32 | tf_op jit(solution)/shard_map/psum | solution.py:118
  243.7 1.2 broadcast_divide_fusion
  244.9 0.6 broadcast_select_fusion.3
  (58 shorter events, 0.7 us)
Async XLA Ops:
  7.2 49.4 %copy-start = (f32[50265]{0:T(1024)S(1)}, f32[50265]{0:T(1024)}, u32[]{:S(2)}) copy-start(f32[50265]{0:T(1024)} %param.26) | copy-start | bytes 603184
  7.2 13.5 %copy-start.2 = (f32[1024]{0:T(1024)S(1)}, f32[1024]{0:T(1024)}, u32[]{:S(2)}) copy-start(f32[1024]{0:T(1024)} %param.32) | copy-start | bytes 12292
  7.2 13.5 %copy-start.3 = (f32[1024]{0:T(1024)S(1)}, f32[1024]{0:T(1024)}, u32[]{:S(2)}) copy-start(f32[1024]{0:T(1024)} %param.31) | copy-start | bytes 12292
  7.2 96.7 %all-gather.6.cloned.1.call-start = ((), (), s32[]{:S(2)}) async-start(), calls=%async_computation.1 | async-start | bytes 2359296 | tf_op jit(solution)/shard_map/all_gather | solution.py:65
  20.5 1.7 copy-start.7
  20.5 1.7 copy-start.8
  20.5 1.7 copy-start.9
  21.9 147.4 %all-gather.4.cloned.1.call-start = ((), (), s32[]{:S(2)}) async-start(), calls=%async_computation | async-start | bytes 17825792 | tf_op jit(solution)/shard_map/all_gather | solution.py:88
  53.7 2.8 %copy-start.6 = (s32[1,1,128]{2,1,0:T(1,128)S(1)}, s32[1,1,128]{2,1,0:T(1,128)}, u32[]{:S(2)}) copy-start(s32[1,1,128]{2,1,0:T(1,128)} %param.22) | copy-start | bytes 1540
  53.7 14.9 %copy-start.10 = (s32[1,1,32]{2,1,0:T(1,128)S(1)}, s32[1,1,32]{2,1,0:T(1,128)}, u32[]{:S(2)}) copy-start(s32[1,1,32]{2,1,0:T(1,128)} %param.34) | copy-start | bytes 388
  55.2 16.5 %copy-start.1 = (s32[1,1,32]{2,1,0:T(1,128)S(1)}, s32[1,1,32]{2,1,0:T(1,128)}, u32[]{:S(2)}) copy-start(s32[1,1,32]{2,1,0:T(1,128)} %param.33) | copy-start | bytes 388
  55.2 17.2 %copy-start.4 = (s32[4,1,128]{2,1,0:T(1,128)S(1)}, s32[4,1,128]{2,1,0:T(1,128)}, u32[]{:S(2)}) copy-start(s32[4,1,128]{2,1,0:T(1,128)} %param.23) | copy-start | bytes 6148
  55.2 20.3 %copy-start.5 = (s32[4,1]{0,1:T(1,128)S(1)}, s32[4,1]{0,1:T(1,128)}, u32[]{:S(2)}) copy-start(s32[4,1]{0,1:T(1,128)} %param.25) | copy-start | bytes 52
Sparse Core Ops, SparseCore 0:
  22.0 27.6 all-gather.5
  55.3 113.9 all-gather.3
